TPU v7x, 32 devices: a whole 2x2x4 slice. The times are simulated.
32 devices in a mesh: groups: 2 (over y), expert: 4 (over z), dp: 2 (over x), inner: 2 (over core).
Axes of the slice: x: 2, y: 2, z: 4, core: 2. Of those that a mesh axis runs over, the one named last changes fastest.
Arguments:
- tokens: bfloat16 [2048, 1536], P(('groups', 'expert', 'dp'), 'inner'), parts along dimension 0, may hold values from -6 to 6
- out_grad: bfloat16 [2048, 1536], P(('groups', 'expert', 'dp'), 'inner'), parts along dimension 0, may hold values from -6 to 6
- expert_ids: int32 [2048, 8], P(('groups', 'expert', 'dp')), parts along dimension 0, may hold values from 0 to 63, all different within a row; in each aligned block of 128 rows (0 to 127, 128 to 255, ...) at most 17 rows name the same one
- gate_probs: float32 [2048, 8], P(('groups', 'expert', 'dp')), parts along dimension 0, may hold values from 0.05 to 0.5
- gate_weight: bfloat16 [64, 1536, 384], P('expert', 'inner', 'dp'), may hold values from -0.15625 to 0.15625
- up_weight: bfloat16 [64, 1536, 384], P('expert', 'inner', 'dp'), may hold values from -0.15625 to 0.15625
- down_weight: bfloat16 [64, 384, 1536], P('expert', 'dp', 'inner'), may hold values from -0.3125 to 0.3125
Outputs:
- token_grad: bfloat16 [2048, 1536], P(('groups', 'expert', 'dp'), 'inner'), parts along dimension 0
- prob_grad: float32 [2048, 8], P(('groups', 'expert', 'dp')), parts along dimension 0
- gate_weight_grad: bfloat16 [128, 1536, 384], P(('groups', 'expert'), 'inner', 'dp'), parts along dimension 0
- up_weight_grad: bfloat16 [128, 1536, 384], P(('groups', 'expert'), 'inner', 'dp'), parts along dimension 0
- down_weight_grad: bfloat16 [128, 384, 1536], P(('groups', 'expert'), 'dp', 'inner'), parts along dimension 0
There are 2 independent parts, one for each index of `groups`. A program takes and returns all parts, laid end to end along the dimension named above; an argument that names none is the same for every part. Nothing has to cross between parts.
Inputs may be any that keep to these rules, and one draw needn't show every extreme that they name: `expert_ids`: within the rows of one block of 128 tokens no expert is chosen more than 17 times, and some expert is chosen exactly 17 times in some block; a token's 8 experts differ.
All inputs are finite; a program needn't handle non-finite values.
Results may differ from a plain program's by a relative error of at most 0.015.
Values may be sent and summed in bfloat16 or wider, within the bound.
A program may use at most 192 MiB of HBM per device.

v0:
```python
import jax
import jax.numpy as jnp
from jax import lax
from jax.sharding import PartitionSpec as P


def on_device(tokens, out_grad, expert_ids, gate_probs, gate_weight, up_weight, down_weight):
    tok_rows, width_half = tokens.shape
    top_count = expert_ids.shape[1]
    per_dev = gate_weight.shape[0]
    owners = lax.axis_size("expert")
    experts = per_dev * owners
    capacity = tok_rows * top_count // experts + 1
    row_count = owners * capacity
    total_slots = experts * capacity
    pair_count = tok_rows * top_count
    chosen = expert_ids.reshape(-1)
    matches = (chosen[:, None] == jnp.arange(experts, dtype=jnp.int32)[None, :]).astype(jnp.int32)
    before = jnp.cumsum(matches, axis=0) - matches
    slot_index = jnp.sum(before * matches, axis=1)
    target = chosen % per_dev * row_count + chosen // per_dev * capacity + slot_index
    source_tok = (
        jnp.zeros((total_slots,), jnp.int32)
        .at[target]
        .set(jnp.arange(pair_count, dtype=jnp.int32) // top_count)
    )
    filled = jnp.zeros((total_slots,), jnp.bfloat16).at[target].set(1)
    slot_probs = (
        jnp.zeros((total_slots,), jnp.float32)
        .at[target]
        .set(gate_probs.reshape(-1))
        .astype(jnp.bfloat16)
    )
    sent_rows = (tokens[source_tok] * filled[:, None]).reshape(
        per_dev, owners, capacity, width_half
    )
    sent_grads = (out_grad[source_tok] * filled[:, None]).reshape(
        per_dev, owners, capacity, width_half
    )
    sent_probs = slot_probs.reshape(per_dev, owners, capacity)
    arrived_rows, arrived_grads, arrived_probs = (
        lax.all_to_all(sent_rows, "expert", split_axis=1, concat_axis=1, tiled=True),
        lax.all_to_all(sent_grads, "expert", split_axis=1, concat_axis=1, tiled=True),
        lax.all_to_all(sent_probs, "expert", split_axis=1, concat_axis=1, tiled=True),
    )
    full_gate, full_up, full_down = (
        lax.all_gather(gate_weight, "dp", axis=2, tiled=True),
        lax.all_gather(up_weight, "dp", axis=2, tiled=True),
        lax.all_gather(down_weight, "dp", axis=1, tiled=True),
    )
    expert_rows = arrived_rows.reshape(per_dev, row_count, width_half)
    gate_part = jnp.einsum(
        "jrd,jdf->jrf", expert_rows, full_gate, preferred_element_type=jnp.float32
    )
    up_part = jnp.einsum("jrd,jdf->jrf", expert_rows, full_up, preferred_element_type=jnp.float32)
    gate_sum, up_sum = (
        lax.psum(gate_part.astype(jnp.bfloat16), "inner").astype(jnp.float32),
        lax.psum(up_part.astype(jnp.bfloat16), "inner").astype(jnp.float32),
    )
    sigmoid_gate = jax.nn.sigmoid(gate_sum)
    activated = gate_sum * sigmoid_gate
    hidden = (activated * up_sum).astype(jnp.bfloat16)
    expert_grads = arrived_grads.reshape(per_dev, row_count, width_half)
    prob_col = arrived_probs.reshape(per_dev, row_count, 1).astype(jnp.float32)
    slope_part = jnp.einsum(
        "jrd,jfd->jrf", expert_grads, full_down, preferred_element_type=jnp.float32
    )
    slope_sum = lax.psum(slope_part.astype(jnp.bfloat16), "inner").astype(jnp.float32)
    scores = jnp.sum(hidden.astype(jnp.float32) * slope_sum, axis=-1)
    hidden_grad = prob_col * slope_sum
    gate_back = (
        hidden_grad * up_sum * sigmoid_gate * (1.0 + gate_sum * (1.0 - sigmoid_gate))
    ).astype(jnp.bfloat16)
    up_back = (hidden_grad * activated).astype(jnp.bfloat16)
    row_grads = jnp.einsum("jrf,jdf->jrd", gate_back, full_gate, preferred_element_type=jnp.float32)
    row_grads = (
        row_grads + jnp.einsum("jrf,jdf->jrd", up_back, full_up, preferred_element_type=jnp.float32)
    ).astype(jnp.bfloat16)
    returned_rows, returned_scores = (
        lax.all_to_all(
            row_grads.reshape(per_dev, owners, capacity, width_half),
            "expert",
            split_axis=1,
            concat_axis=1,
            tiled=True,
        ),
        lax.all_to_all(
            scores.astype(jnp.bfloat16).reshape(per_dev, owners, capacity),
            "expert",
            split_axis=1,
            concat_axis=1,
            tiled=True,
        ),
    )
    pair_rows = returned_rows.reshape(total_slots, width_half)[target]
    token_grad = jnp.sum(
        pair_rows.reshape(tok_rows, top_count, width_half).astype(jnp.float32), axis=1
    ).astype(jnp.bfloat16)
    prob_grad = returned_scores.reshape(-1)[target].astype(jnp.float32).reshape(tok_rows, top_count)
    grad_gate = jnp.einsum(
        "jrd,jrf->jdf", expert_rows, gate_back, preferred_element_type=jnp.float32
    )
    grad_up = jnp.einsum("jrd,jrf->jdf", expert_rows, up_back, preferred_element_type=jnp.float32)
    down_rows = (prob_col * expert_grads).astype(jnp.bfloat16)
    grad_down = jnp.einsum("jrf,jrd->jfd", hidden, down_rows, preferred_element_type=jnp.float32)
    summed_gate, summed_up, summed_down = (
        lax.psum_scatter(
            grad_gate.astype(jnp.bfloat16), "dp", scatter_dimension=2, tiled=True
        ).astype(jnp.float32),
        lax.psum_scatter(
            grad_up.astype(jnp.bfloat16), "dp", scatter_dimension=2, tiled=True
        ).astype(jnp.float32),
        lax.psum_scatter(
            grad_down.astype(jnp.bfloat16), "dp", scatter_dimension=1, tiled=True
        ).astype(jnp.float32),
    )
    return (
        token_grad,
        prob_grad,
        summed_gate.astype(jnp.bfloat16),
        summed_up.astype(jnp.bfloat16),
        summed_down.astype(jnp.bfloat16),
    )


def solution(mesh):
    placed = (
        P(("groups", "expert", "dp"), "inner"),
        P(("groups", "expert", "dp"), "inner"),
        P(("groups", "expert", "dp"), None),
        P(("groups", "expert", "dp"), None),
        P("expert", "inner", "dp"),
        P("expert", "inner", "dp"),
        P("expert", "dp", "inner"),
    )
    return jax.shard_map(
        on_device,
        mesh=mesh,
        in_specs=placed,
        out_specs=(
            P(("groups", "expert", "dp"), "inner"),
            P(("groups", "expert", "dp"), None),
            P(("groups", "expert"), "inner", "dp"),
            P(("groups", "expert"), "inner", "dp"),
            P(("groups", "expert"), "dp", "inner"),
        ),
        check_vma=False,
    )
```

profile of v0, /device:TPU:0, one launch (start us, length us, event | category | flops | bytes accessed | tf_op | source)
XLA Modules:
  0.0 753.5 jit_solution(1835674188766818200)
XLA Ops:
  7.2 0.7 all-gather.6.cloned.1.call-update
  8.0 0.7 all-gather.8.cloned.1.call-update
  8.7 0.7 all-gather.4.cloned.1.call-update
  9.4 0.1 copy.48
  9.5 0.1 eq.31
  9.7 0.1 reshape.205
  9.8 18.0 %reduce-window.6 = s32[64,8,128]{2,1,0:T(8,128)S(1)} reduce-window(s32[64,8,128]{2,1,0:T(8,128)S(1)} %fusion.24, s32[]{:T(128)} %constant.51.clone.1), window={size=1x1x128 pad=0_0x0_0x127_0}, to_apply=%region_0.0 | reduce-window | flops 8323072 | bytes 524292 | tf_op jit(solution)/shard_map/reduce-window
  27.8 0.1 slice.16
  28.0 0.1 copy.51
  28.3 0.1 broadcast_add_fusion
  28.5 4.3 scatter_custom_fusion.1
  32.9 4.8 gather_fusion.1
  37.7 2.5 gather.19
  40.2 7.6 %scatter_custom_fusion.2 = bf16[1088]{0:T(1024)(128)(2,1)S(1)} fusion(s32[1024]{0:T(1024)S(1)} %bitcast.54, bf16[1024]{0:T(1024)(128)(2,1)S(1)} %broadcast.149, bf16[]{:T(256)} %constant.63.clone.1), kind=kCustom, calls=%fused_computation.74 | custom fusion | bytes 2178 | tf_op jit(solution)/shard_map/scatter | solution.py:27
  47.8 0.1 mul.93
  48.0 4.8 gather_fusion
  52.8 3.6 gather.17
  56.4 3.4 broadcast_multiply_fusion
  59.8 2.1 copy.58
  61.9 6.3 all-to-all-start.2
  68.3 3.8 copy.56
  72.1 35.3 %all-to-all-done.2 = bf16[16,4,17,768]{3,0,2,1:T(8,128)(2,1)S(1)} async-done(((bf16[16,4,17,768]{3,0,2,1:T(8,128)(2,1)}), bf16[16,4,17,768]{3,0,2,1:T(8,128)(2,1)S(1)}, u32[]{:S(2)}, u32[]{:S(2)}) %all-to-all-start.2) | async-done | bytes 1671200 | tf_op jit(solution)/shard_map/all_to_all | solution.py:42
  107.3 3.6 all-to-all-start.1
  110.9 0.5 all-reduce.3.cloned.1.call-start
  111.4 18.8 %all-gather.6.cloned.1.call-done = bf16[16,768,384]{1,2,0:T(8,128)(2,1)} async-done(((bf16[16,768,192]{1,2,0:T(8,128)(2,1)}), bf16[16,768,384]{1,2,0:T(8,128)(2,1)}) %all-gather.6.cloned.1.call-update) | async-done | bytes 9437200 | tf_op jit(solution)/shard_map/all_gather | solution.py:48
  130.2 7.4 convolution_convert_fusion.4
  137.7 112.2 %all-gather.8.cloned.1.call-done = bf16[16,768,384]{1,2,0:T(8,128)(2,1)} async-done(((bf16[16,768,192]{1,2,0:T(8,128)(2,1)}), bf16[16,768,384]{1,2,0:T(8,128)(2,1)}) %all-gather.8.cloned.1.call-update) | async-done | bytes 9437200 | tf_op jit(solution)/shard_map/all_gather | solution.py:47
  249.8 7.5 convolution_convert_fusion.3
  257.3 112.0 %all-gather.4.cloned.1.call-done = bf16[16,384,768]{2,1,0:T(8,128)(2,1)} async-done(((bf16[16,192,768]{2,1,0:T(8,128)(2,1)}), bf16[16,384,768]{2,1,0:T(8,128)(2,1)}) %all-gather.4.cloned.1.call-update) | async-done | bytes 9437200 | tf_op jit(solution)/shard_map/all_gather | solution.py:49
  369.3 7.5 fusion.14
  376.9 0.6 copy-done.6
  377.5 0.1 copy.53
  377.7 4.3 scatter_custom_fusion
  382.0 0.1 reshape.208
  382.2 0.1 reshape.281
  382.3 10.0 %all_to_all.25 = bf16[4,2,136]{2,1,0:T(2,128)(2,1)S(1)} all-to-all(bf16[4,2,136]{2,1,0:T(2,128)(2,1)S(1)} %reshape.281), channel_id=1, replica_groups=mesh['groups'=2,'expert'=4,'dp'=2,'inner'=2] {'expert'}, dimensions={0} | all-to-all | bytes 4352 | tf_op jit(solution)/shard_map/all_to_all | solution.py:44
  392.5 7.0 all-reduce.3.cloned.1.call-done
  399.5 8.3 %convolution_convert_fusion.2 = bf16[16,768,384]{1,2,0:T(8,128)(2,1)} fusion(bf16[16,68,768]{2,0,1:T(8,128)(2,1)S(1)} %bitcast.41, bf16[16,68,384]{2,1,0:T(8,128)(2,1)} %get-tuple-element.21, bf16[16,68,384]{2,1,0:T(8,128)(2,1)} %get-tuple-element.20, bf16[16,68,384]{2,1,0:T(8,128)(2,1)} %get-tuple-element.22, f32[16,68]{1,0:T(8,128)S(1)} %reshape.215), kind=kOutput, calls=%fused_computation.9 | convolution fusion | flops 652296192 | bytes 13619456 | tf_op jit(solution)/shard_map/jrd,jrf->jdf/dot_general | solution.py:100
  407.8 0.2 reduce-scatter.6.cloned.1.call-start
  408.0 8.2 %convolution_convert_fusion.1 = bf16[16,768,384]{1,2,0:T(8,128)(2,1)} fusion(bf16[16,68,768]{2,0,1:T(8,128)(2,1)S(1)} %bitcast.42, bf16[16,68,384]{2,1,0:T(8,128)(2,1)} %get-tuple-element.20, f32[16,68]{1,0:T(8,128)S(1)} %reshape.215, bf16[16,68,384]{2,1,0:T(8,128)(2,1)} %get-tuple-element.22), kind=kOutput, calls=%fused_computation.8 | convolution fusion | flops 650207232 | bytes 12783872 | tf_op jit(solution)/shard_map/jrd,jrf->jdf/dot_general | solution.py:103
  416.3 0.1 copy.67
  416.4 0.4 multiply_convert_fusion
  416.8 0.7 copy-done.4
  417.4 7.6 %convolution_convert_fusion = bf16[16,384,768]{2,1,0:T(8,128)(2,1)} fusion(bf16[16,68,768]{2,0,1:T(8,128)(2,1)S(1)} %multiply_convert_fusion, bf16[16,68,384]{2,1,0:T(8,128)(2,1)} %get-tuple-element.21, bf16[16,68,384]{2,1,0:T(8,128)(2,1)S(1)} %copy-done.4), kind=kOutput, calls=%fused_computation.7 | convolution fusion | flops 649789440 | bytes 12779520 | tf_op jit(solution)/shard_map/jrf,jrd->jfd/dot_general | solution.py:105
  425.0 1.2 copy-done.3
  426.2 2.1 fusion.2
  428.3 0.7 reshape.283
  429.0 4.8 all-to-all-start.4
  433.9 6.1 fusion.41
  440.0 0.6 slice-done.2
  440.6 2.0 add_convert_fusion
  442.6 1.5 copy.61
  444.1 5.3 all-to-all-start.3
  449.5 0.1 reshape.214
  449.7 6.8 gather_fusion.3
  456.6 0.7 copy.69
  457.2 31.1 %all-to-all-done.3 = bf16[16,4,17,768]{3,0,2,1:T(8,128)(2,1)S(1)} async-done(((bf16[16,4,17,768]{3,0,2,1:T(8,128)(2,1)}), bf16[16,4,17,768]{3,0,2,1:T(8,128)(2,1)S(1)}, u32[]{:S(2)}, u32[]{:S(2)}) %all-to-all-start.3) | async-done | bytes 1671200 | tf_op jit(solution)/shard_map/all_to_all | solution.py:80
  488.3 2.1 copy.62
  490.4 2.7 reshape.212
  493.1 4.0 gather_fusion.2
  497.1 1.7 bitcast_reduce_fusion
  498.8 20.8 %reduce-scatter.4.cloned.1.call-done = bf16[16,768,192]{1,2,0:T(8,128)(2,1)} async-done(((bf16[16,768,384]{1,2,0:T(8,128)(2,1)}), bf16[16,768,192]{1,2,0:T(8,128)(2,1)}) %reduce-scatter.4.cloned.1.call-update) | async-done | bytes 4718608 | tf_op jit(solution)/shard_map/reduce_scatter | solution.py:107
  519.6 113.3 %reduce-scatter.6.cloned.1.call-done = bf16[16,768,192]{1,2,0:T(8,128)(2,1)} async-done(((bf16[16,768,384]{1,2,0:T(8,128)(2,1)}), bf16[16,768,192]{1,2,0:T(8,128)(2,1)}) %reduce-scatter.6.cloned.1.call-update) | async-done | bytes 4718608 | tf_op jit(solution)/shard_map/reduce_scatter | solution.py:110
  633.0 113.5 %reduce-scatter.8.cloned.1.call-done = bf16[16,192,768]{2,1,0:T(8,128)(2,1)} async-done(((bf16[16,384,768]{2,1,0:T(8,128)(2,1)}), bf16[16,192,768]{2,1,0:T(8,128)(2,1)}) %reduce-scatter.8.cloned.1.call-update) | async-done | bytes 4718608 | tf_op jit(solution)/shard_map/reduce_scatter | solution.py:113
  (51 shorter events, 1.2 us)
Async XLA Ops:
  7.2 25.7 %copy-start = (bf16[128,768]{1,0:T(8,128)(2,1)S(1)}, bf16[128,768]{1,0:T(8,128)(2,1)}, u32[]{:S(2)}) copy-start(bf16[128,768]{1,0:T(8,128)(2,1)} %param.7) | copy-start | bytes 589828
  7.2 123.1 %all-gather.6.cloned.1.call-start = ((), (), s32[]{:S(2)}) async-start(), calls=%async_computation.9 | async-start | bytes 14155776 | tf_op jit(solution)/shard_map/all_gather | solution.py:48
  7.9 241.9 %all-gather.8.cloned.1.call-start = ((), (), s32[]{:S(2)}) async-start(), calls=%async_computation.10 | async-start | bytes 14155776 | tf_op jit(solution)/shard_map/all_gather | solution.py:47
  8.7 0.7 copy-start.5
  8.7 360.6 %all-gather.4.cloned.1.call-start = ((), (), s32[]{:S(2)}) async-start(), calls=%async_computation.8 | async-start | bytes 14155776 | tf_op jit(solution)/shard_map/all_gather | solution.py:49
  37.7 10.3 %copy-start.2 = (bf16[128,768]{1,0:T(8,128)(2,1)S(1)}, bf16[128,768]{1,0:T(8,128)(2,1)}, u32[]{:S(2)}) copy-start(bf16[128,768]{1,0:T(8,128)(2,1)} %param.8) | copy-start | bytes 589828
  61.9 45.4 %all-to-all-start.2 = ((bf16[16,4,17,768]{3,0,2,1:T(8,128)(2,1)}), bf16[16,4,17,768]{3,0,2,1:T(8,128)(2,1)S(1)}, u32[]{:S(2)}, u32[]{:S(2)}) async-start(bf16[16,4,17,768]{3,0,2,1:T(8,128)(2,1)} %copy.58), calls=%async_computation.2 | async-start | bytes 3342336 | tf_op jit(solution)/shard_map/all_to_all | solution.py:42
  107.3 150.0 %all-to-all-start.1 = ((bf16[16,4,17,768]{3,0,2,1:T(8,128)(2,1)}), bf16[16,4,17,768]{3,0,2,1:T(8,128)(2,1)S(1)}, u32[]{:S(2)}, u32[]{:S(2)}) async-start(bf16[16,4,17,768]{3,0,2,1:T(8,128)(2,1)} %copy.56), calls=%async_computation.1 | async-start | bytes 3342336 | tf_op jit(solution)/shard_map/all_to_all | solution.py:43
  110.9 288.5 %all-reduce.3.cloned.1.call-start = ((), (), s32[]{:S(2)}) async-start(), calls=%async_computation.14 | async-start | bytes 5308416 | tf_op jit(solution)/shard_map/psum | solution.py:68
  376.8 0.7 copy-start.6
  376.8 142.8 %reduce-scatter.4.cloned.1.call-start = ((), (), s32[]{:S(2)}) async-start(), calls=%async_computation.11 | async-start | bytes 14155776 | tf_op jit(solution)/shard_map/reduce_scatter | solution.py:107
  407.8 225.2 %reduce-scatter.6.cloned.1.call-start = ((), (), s32[]{:S(2)}) async-start(), calls=%async_computation.12 | async-start | bytes 14155776 | tf_op jit(solution)/shard_map/reduce_scatter | solution.py:110
  416.2 1.2 copy-start.4
  416.2 330.2 %reduce-scatter.8.cloned.1.call-start = ((), (), s32[]{:S(2)}) async-start(), calls=%async_computation.13 | async-start | bytes 14155776 | tf_op jit(solution)/shard_map/reduce_scatter | solution.py:113
  425.0 1.2 copy-start.3
  426.2 13.8 %slice-start = ((s8[9437184]{0:T(1024)(128)(4,1)}), s8[1048576]{0:T(1024)(128)(4,1)S(1)}, s32[]{:S(2)}) async-start(s8[9437184]{0:T(1024)(128)(4,1)} %bitcast.44), calls=%async_computation.15 | async-start | bytes 2097152
  429.0 15.0 %all-to-all-start.4 = ((bf16[4,2,136]{2,1,0:T(2,128)(2,1)}), bf16[4,2,136]{2,1,0:T(2,128)(2,1)S(1)}, u32[]{:S(2)}, u32[]{:S(2)}) async-start(bf16[4,2,136]{2,1,0:T(2,128)(2,1)} %reshape.283), calls=%async_computation.4 | async-start | bytes 8192 | tf_op jit(solution)/shard_map/all_to_all | solution.py:87
  433.9 6.1 slice-start.1
  433.9 6.7 slice-start.2
  444.1 44.2 %all-to-all-start.3 = ((bf16[16,4,17,768]{3,0,2,1:T(8,128)(2,1)}), bf16[16,4,17,768]{3,0,2,1:T(8,128)(2,1)S(1)}, u32[]{:S(2)}, u32[]{:S(2)}) async-start(bf16[16,4,17,768]{3,0,2,1:T(8,128)(2,1)} %bitcast.6), calls=%async_computation.3 | async-start | bytes 3342336 | tf_op jit(solution)/shard_map/all_to_all | solution.py:80
  493.1 253.4 %copy-start.1 = (bf16[128,768]{1,0:T(8,128)(2,1)S(1)}, bf16[128,768]{1,0:T(8,128)(2,1)}, u32[]{:S(2)}) copy-start(bf16[128,768]{1,0:T(8,128)(2,1)} %param.7) | copy-start | bytes 589828
Sparse Core Ops, SparseCore 0:
  9.6 120.6 all-gather.5
  131.8 117.9 all-gather.7
  251.4 117.8 all-gather.3
  376.9 22.4 all-reduce.2
  407.9 111.6 reduce-scatter.3
  522.4 110.5 reduce-scatter.5
  635.9 110.5 reduce-scatter.7
where the time goes:
time: 762 us; the launch traced here: 754 us
  waiting for transfers between devices  566 us (74%)
  local copies, waits for them, and re-layouts  61.4 us (8%)
  matrix products  54.5 us (7%)
  other arithmetic  25.9 us (3%)
  starting transfers between devices  20.9 us (3%)
  between operations  14.7 us (2%)
  blocking collectives  10 us (1%)
    reduce_scatter x1, waiting for transfers between devices, on_device(): lax.psum_scatter(grad_down.astype(jnp.bfloat16), 'dp', scatter_dimension=...  113 us
    reduce_scatter x1, waiting for transfers between devices, on_device(): lax.psum_scatter(grad_up.astype(jnp.bfloat16), 'dp', scatter_dimension=2,...  113 us
    all_gather x1, waiting for transfers between devices, on_device(): lax.all_gather(gate_weight, 'dp', axis=2, tiled=True)  112 us
    all_gather x1, waiting for transfers between devices, on_device(): lax.all_gather(down_weight, 'dp', axis=1, tiled=True)  112 us
    all_to_all x1, waiting for transfers between devices, on_device(): lax.all_to_all(sent_rows, 'expert', split_axis=1, concat_axis=1, tiled=True)  35.3 us
    all_to_all x1, waiting for transfers between devices, on_device(): lax.all_to_all(row_grads.reshape(per_dev, owners, capacity, width_half),...  31.1 us
    reduce_scatter x1, waiting for transfers between devices, on_device(): lax.psum_scatter(grad_gate.astype(jnp.bfloat16), 'dp', scatter_dimension=...  20.8 us
    all_gather x1, waiting for transfers between devices, on_device(): lax.all_gather(up_weight, 'dp', axis=2, tiled=True)  18.8 us
  transfers between devices with their start and end apart: 11, of which 9 were waited for; matrix products, arithmetic and copies ran while one was open for 16% of the time, Pallas kernels for 0%

commit v1 on v0

--- a/solution.py
+++ b/solution.py
@@ -2,6 +2,29 @@
 import jax.numpy as jnp
 from jax import lax
 from jax.sharding import PartitionSpec as P
+
+
+def cut_along(x, dim, devices):
+    lengths = x.shape
+    blocks = x.reshape(*lengths[:dim], devices, lengths[dim] // devices, *lengths[dim + 1 :])
+    return jnp.moveaxis(blocks, dim, 0)
+
+
+def joined_along(blocks, dim):
+    blocks = jnp.moveaxis(blocks, 0, dim)
+    shape = blocks.shape
+    return blocks.reshape(*shape[:dim], shape[dim] * shape[dim + 1], *shape[dim + 2 :])
+
+
+def sent_to_each(shard, axis, split_dim, concat_dim):
+    devices, index = (lax.axis_size(axis), lax.axis_index(axis))
+    parts = cut_along(shard, split_dim, devices)
+    outs = [parts[index]]
+    for step in range(1, devices):
+        sent = parts[(index + step) % devices]
+        outs.append(lax.ppermute(sent, axis, [(i, (i + step) % devices) for i in range(devices)]))
+    parts = jnp.stack(outs)[(index - jnp.arange(devices)) % devices]
+    return joined_along(parts, concat_dim)
 
 
 def on_device(tokens, out_grad, expert_ids, gate_probs, gate_weight, up_weight, down_weight):
@@ -77,13 +100,7 @@
         row_grads + jnp.einsum("jrf,jdf->jrd", up_back, full_up, preferred_element_type=jnp.float32)
     ).astype(jnp.bfloat16)
     returned_rows, returned_scores = (
-        lax.all_to_all(
-            row_grads.reshape(per_dev, owners, capacity, width_half),
-            "expert",
-            split_axis=1,
-            concat_axis=1,
-            tiled=True,
-        ),
+        sent_to_each(row_grads.reshape(per_dev, owners, capacity, width_half), "expert", 1, 1),
         lax.all_to_all(
             scores.astype(jnp.bfloat16).reshape(per_dev, owners, capacity),
             "expert",

time: 762 us -> 762 us (level)
    all_to_all x1 -> x0, waiting for transfers between devices: 31.1 us -> none  [on_device(): lax.all_to_all(row_grads.reshape(per_dev, owners, capacity, width_half),...]
    all_to_all x1, waiting for transfers between devices: 0.01 us -> 29.7 us  [on_device(): lax.all_to_all(scores.astype(jnp.bfloat16).reshape(per_dev, owners, capac...]
    another operation x3 -> x4, other arithmetic: 18.2 us -> 19.5 us
  transfers between devices with their start and end apart: 11 -> 13, of which waited for: 9 -> 9; matrix products, arithmetic and copies ran while one was open for 16% -> 16% of each run, Pallas kernels for 0% -> 0%
where the time goes in v1:
time: 762 us; the launch traced here: 753 us
  waiting for transfers between devices  565 us (74%)
  local copies, waits for them, and re-layouts  63.1 us (8%)
  matrix products  54.4 us (7%)
  other arithmetic  26 us (3%)
  starting transfers between devices  19.7 us (3%)
  between operations  14.7 us (2%)
  blocking collectives  10 us (1%)
    reduce_scatter x1, waiting for transfers between devices, on_device(): lax.psum_scatter(grad_down.astype(jnp.bfloat16), 'dp', scatter_dimension=...  113 us
    reduce_scatter x1, waiting for transfers between devices, on_device(): lax.psum_scatter(grad_up.astype(jnp.bfloat16), 'dp', scatter_dimension=2,...  113 us
    all_gather x1, waiting for transfers between devices, on_device(): lax.all_gather(gate_weight, 'dp', axis=2, tiled=True)  112 us
    all_gather x1, waiting for transfers between devices, on_device(): lax.all_gather(down_weight, 'dp', axis=1, tiled=True)  112 us
    all_to_all x1, waiting for transfers between devices, on_device(): lax.all_to_all(sent_rows, 'expert', split_axis=1, concat_axis=1, tiled=True)  35.3 us
    all_to_all x1, waiting for transfers between devices, on_device(): lax.all_to_all(scores.astype(jnp.bfloat16).reshape(per_dev, owners, capac...  29.7 us
    reduce_scatter x1, waiting for transfers between devices, on_device(): lax.psum_scatter(grad_gate.astype(jnp.bfloat16), 'dp', scatter_dimension=...  21.6 us
    all_gather x1, waiting for transfers between devices, on_device(): lax.all_gather(up_weight, 'dp', axis=2, tiled=True)  18.8 us
  transfers between devices with their start and end apart: 13, of which 9 were waited for; matrix products, arithmetic and copies ran while one was open for 16% of the time, Pallas kernels for 0%

profile of v1, /device:TPU:0, one launch (start us, length us, event | category | flops | bytes accessed | tf_op | source)
XLA Modules:
  0.0 753.4 jit_solution(9461595209076878775)
XLA Ops:
  7.2 0.7 all-gather.6.cloned.1.call-update
  8.0 0.7 all-gather.8.cloned.1.call-update
  8.7 0.7 all-gather.4.cloned.1.call-update
  9.8 18.0 %reduce-window.6 = s32[64,8,128]{2,1,0:T(8,128)S(1)} reduce-window(s32[64,8,128]{2,1,0:T(8,128)S(1)} %fusion.24, s32[]{:T(128)} %constant.85.clone.1), window={size=1x1x128 pad=0_0x0_0x127_0}, to_apply=%region_0.0 | reduce-window | flops 8323072 | bytes 524292 | tf_op jit(solution)/shard_map/reduce-window
  27.8 0.1 slice.18
  28.0 0.1 copy.51
  28.3 0.1 broadcast_add_fusion
  28.5 4.3 scatter_custom_fusion.1
  32.9 4.8 gather_fusion.1
  37.7 2.5 gather.22
  40.2 7.6 %scatter_custom_fusion.2 = bf16[1088]{0:T(1024)(128)(2,1)S(1)} fusion(s32[1024]{0:T(1024)S(1)} %bitcast.78, bf16[1024]{0:T(1024)(128)(2,1)S(1)} %broadcast.222, bf16[]{:T(256)} %constant.97.clone.1), kind=kCustom, calls=%fused_computation.84 | custom fusion | bytes 2178 | tf_op jit(solution)/shard_map/scatter | solution.py:50
  47.8 0.1 mul.93
  48.0 4.8 gather_fusion
  52.8 3.6 gather.20
  56.4 3.4 broadcast_multiply_fusion
  59.8 2.1 copy.58
  61.9 6.3 all-to-all-start.2
  68.3 3.8 copy.56
  72.1 35.3 %all-to-all-done.2 = bf16[16,4,17,768]{3,0,2,1:T(8,128)(2,1)S(1)} async-done(((bf16[16,4,17,768]{3,0,2,1:T(8,128)(2,1)}), bf16[16,4,17,768]{3,0,2,1:T(8,128)(2,1)S(1)}, u32[]{:S(2)}, u32[]{:S(2)}) %all-to-all-start.2) | async-done | bytes 1671200 | tf_op jit(solution)/shard_map/all_to_all | solution.py:65
  107.3 3.6 all-to-all-start.1
  110.9 0.5 all-reduce.3.cloned.1.call-start
  111.4 18.8 %all-gather.6.cloned.1.call-done = bf16[16,768,384]{1,2,0:T(8,128)(2,1)} async-done(((bf16[16,768,192]{1,2,0:T(8,128)(2,1)}), bf16[16,768,384]{1,2,0:T(8,128)(2,1)}) %all-gather.6.cloned.1.call-update) | async-done | bytes 9437200 | tf_op jit(solution)/shard_map/all_gather | solution.py:71
  130.2 7.4 convolution_convert_fusion.4
  137.7 112.2 %all-gather.8.cloned.1.call-done = bf16[16,768,384]{1,2,0:T(8,128)(2,1)} async-done(((bf16[16,768,192]{1,2,0:T(8,128)(2,1)}), bf16[16,768,384]{1,2,0:T(8,128)(2,1)}) %all-gather.8.cloned.1.call-update) | async-done | bytes 9437200 | tf_op jit(solution)/shard_map/all_gather | solution.py:70
  249.8 7.5 convolution_convert_fusion.3
  257.3 112.0 %all-gather.4.cloned.1.call-done = bf16[16,384,768]{2,1,0:T(8,128)(2,1)} async-done(((bf16[16,192,768]{2,1,0:T(8,128)(2,1)}), bf16[16,384,768]{2,1,0:T(8,128)(2,1)}) %all-gather.4.cloned.1.call-update) | async-done | bytes 9437200 | tf_op jit(solution)/shard_map/all_gather | solution.py:72
  369.3 7.4 fusion.14
  376.8 0.6 copy-done.8
  377.6 4.3 scatter_custom_fusion
  382.0 0.1 reshape.258
  382.2 10.0 %all_to_all.20 = bf16[4,2,136]{2,1,0:T(2,128)(2,1)S(1)} all-to-all(bf16[4,2,136]{2,1,0:T(2,128)(2,1)S(1)} %reshape.339), channel_id=1, replica_groups=mesh['groups'=2,'expert'=4,'dp'=2,'inner'=2] {'expert'}, dimensions={0} | all-to-all | bytes 4352 | tf_op jit(solution)/shard_map/all_to_all | solution.py:67
  392.4 7.0 all-reduce.3.cloned.1.call-done
  399.4 8.3 %convolution_convert_fusion.2 = bf16[16,768,384]{1,2,0:T(8,128)(2,1)} fusion(bf16[16,68,768]{2,0,1:T(8,128)(2,1)S(1)} %bitcast.61, bf16[16,68,384]{2,1,0:T(8,128)(2,1)} %get-tuple-element.21, bf16[16,68,384]{2,1,0:T(8,128)(2,1)} %get-tuple-element.20, bf16[16,68,384]{2,1,0:T(8,128)(2,1)} %get-tuple-element.22, f32[16,68]{1,0:T(8,128)S(1)} %reshape.263), kind=kOutput, calls=%fused_computation.10 | convolution fusion | flops 652296192 | bytes 13619456 | tf_op jit(solution)/shard_map/jrd,jrf->jdf/dot_general | solution.py:117
  407.7 0.2 reduce-scatter.6.cloned.1.call-start
  407.9 8.2 %convolution_convert_fusion.1 = bf16[16,768,384]{1,2,0:T(8,128)(2,1)} fusion(bf16[16,68,768]{2,0,1:T(8,128)(2,1)S(1)} %bitcast.62, bf16[16,68,384]{2,1,0:T(8,128)(2,1)} %get-tuple-element.20, f32[16,68]{1,0:T(8,128)S(1)} %reshape.263, bf16[16,68,384]{2,1,0:T(8,128)(2,1)} %get-tuple-element.22), kind=kOutput, calls=%fused_computation.9 | convolution fusion | flops 650207232 | bytes 12783872 | tf_op jit(solution)/shard_map/jrd,jrf->jdf/dot_general | solution.py:120
  416.3 0.4 multiply_convert_fusion
  416.7 0.7 copy-done.4
  417.3 7.7 %convolution_convert_fusion = bf16[16,384,768]{2,1,0:T(8,128)(2,1)} fusion(bf16[16,68,768]{2,0,1:T(8,128)(2,1)S(1)} %multiply_convert_fusion, bf16[16,68,384]{2,1,0:T(8,128)(2,1)S(1)} %copy-done.4, bf16[16,68,384]{2,1,0:T(8,128)(2,1)} %get-tuple-element.22), kind=kOutput, calls=%fused_computation.8 | convolution fusion | flops 649789440 | bytes 12779520 | tf_op jit(solution)/shard_map/jrf,jrd->jfd/dot_general | solution.py:122
  425.1 1.1 copy-done.3
  426.2 6.0 fusion.43
  432.2 0.7 slice-done.2
  432.9 0.2 copy-done.5
  433.1 2.0 add_convert_fusion
  435.1 0.3 copy.61
  435.4 1.2 dynamic-slice_bitcast_fusion.3
  436.6 3.6 collective-permute-start.2
  440.1 1.1 collective-permute-start
  441.2 0.8 fusion.2
  442.2 0.7 reshape.341
  442.9 4.2 all-to-all-start.3
  447.1 29.7 %all-to-all-done.3 = bf16[4,2,136]{2,1,0:T(2,128)(2,1)S(1)} async-done(((bf16[4,2,136]{2,1,0:T(2,128)(2,1)}), bf16[4,2,136]{2,1,0:T(2,128)(2,1)S(1)}, u32[]{:S(2)}, u32[]{:S(2)}) %all-to-all-start.3) | async-done | bytes 2208 | tf_op jit(solution)/shard_map/all_to_all | solution.py:104
  476.9 0.1 reshape.262
  477.0 6.8 gather_fusion.4
  483.9 0.7 copy.69
  484.6 0.8 copy-done.6
  485.3 1.3 maximum_bitcast_fusion
  486.7 0.7 gather_fusion.2
  487.3 2.2 copy.62
  489.5 2.7 reshape_reshape.7
  492.2 4.0 gather_fusion.3
  496.2 1.7 bitcast_reduce_fusion
  497.9 21.6 %reduce-scatter.4.cloned.1.call-done = bf16[16,768,192]{1,2,0:T(8,128)(2,1)} async-done(((bf16[16,768,384]{1,2,0:T(8,128)(2,1)}), bf16[16,768,192]{1,2,0:T(8,128)(2,1)}) %reduce-scatter.4.cloned.1.call-update) | async-done | bytes 4718608 | tf_op jit(solution)/shard_map/reduce_scatter | solution.py:124
  519.5 113.3 %reduce-scatter.6.cloned.1.call-done = bf16[16,768,192]{1,2,0:T(8,128)(2,1)} async-done(((bf16[16,768,384]{1,2,0:T(8,128)(2,1)}), bf16[16,768,192]{1,2,0:T(8,128)(2,1)}) %reduce-scatter.6.cloned.1.call-update) | async-done | bytes 4718608 | tf_op jit(solution)/shard_map/reduce_scatter | solution.py:127
  632.9 113.5 %reduce-scatter.8.cloned.1.call-done = bf16[16,192,768]{2,1,0:T(8,128)(2,1)} async-done(((bf16[16,384,768]{2,1,0:T(8,128)(2,1)}), bf16[16,192,768]{2,1,0:T(8,128)(2,1)}) %reduce-scatter.8.cloned.1.call-update) | async-done | bytes 4718608 | tf_op jit(solution)/shard_map/reduce_scatter | solution.py:130
  (64 shorter events, 1.8 us)
Async XLA Ops:
  7.2 25.7 %copy-start = (bf16[128,768]{1,0:T(8,128)(2,1)S(1)}, bf16[128,768]{1,0:T(8,128)(2,1)}, u32[]{:S(2)}) copy-start(bf16[128,768]{1,0:T(8,128)(2,1)} %param.7) | copy-start | bytes 589828
  7.2 123.1 %all-gather.6.cloned.1.call-start = ((), (), s32[]{:S(2)}) async-start(), calls=%async_computation.8 | async-start | bytes 14155776 | tf_op jit(solution)/shard_map/all_gather | solution.py:71
  7.9 241.9 %all-gather.8.cloned.1.call-start = ((), (), s32[]{:S(2)}) async-start(), calls=%async_computation.9 | async-start | bytes 14155776 | tf_op jit(solution)/shard_map/all_gather | solution.py:70
  8.7 0.7 copy-start.7
  8.7 360.6 %all-gather.4.cloned.1.call-start = ((), (), s32[]{:S(2)}) async-start(), calls=%async_computation.7 | async-start | bytes 14155776 | tf_op jit(solution)/shard_map/all_gather | solution.py:72
  37.7 10.3 %copy-start.2 = (bf16[128,768]{1,0:T(8,128)(2,1)S(1)}, bf16[128,768]{1,0:T(8,128)(2,1)}, u32[]{:S(2)}) copy-start(bf16[128,768]{1,0:T(8,128)(2,1)} %param.8) | copy-start | bytes 589828
  61.9 45.4 %all-to-all-start.2 = ((bf16[16,4,17,768]{3,0,2,1:T(8,128)(2,1)}), bf16[16,4,17,768]{3,0,2,1:T(8,128)(2,1)S(1)}, u32[]{:S(2)}, u32[]{:S(2)}) async-start(bf16[16,4,17,768]{3,0,2,1:T(8,128)(2,1)} %copy.58), calls=%async_computation.2 | async-start | bytes 3342336 | tf_op jit(solution)/shard_map/all_to_all | solution.py:65
  107.3 150.0 %all-to-all-start.1 = ((bf16[16,4,17,768]{3,0,2,1:T(8,128)(2,1)}), bf16[16,4,17,768]{3,0,2,1:T(8,128)(2,1)S(1)}, u32[]{:S(2)}, u32[]{:S(2)}) async-start(bf16[16,4,17,768]{3,0,2,1:T(8,128)(2,1)} %copy.56), calls=%async_computation.1 | async-start | bytes 3342336 | tf_op jit(solution)/shard_map/all_to_all | solution.py:66
  110.9 288.5 %all-reduce.3.cloned.1.call-start = ((), (), s32[]{:S(2)}) async-start(), calls=%async_computation.13 | async-start | bytes 5308416 | tf_op jit(solution)/shard_map/psum | solution.py:91
  376.8 0.7 copy-start.8
  376.8 142.8 %reduce-scatter.4.cloned.1.call-start = ((), (), s32[]{:S(2)}) async-start(), calls=%async_computation.10 | async-start | bytes 14155776 | tf_op jit(solution)/shard_map/reduce_scatter | solution.py:124
  407.7 225.2 %reduce-scatter.6.cloned.1.call-start = ((), (), s32[]{:S(2)}) async-start(), calls=%async_computation.11 | async-start | bytes 14155776 | tf_op jit(solution)/shard_map/reduce_scatter | solution.py:127
  416.1 1.2 copy-start.4
  416.2 330.2 %reduce-scatter.8.cloned.1.call-start = ((), (), s32[]{:S(2)}) async-start(), calls=%async_computation.12 | async-start | bytes 14155776 | tf_op jit(solution)/shard_map/reduce_scatter | solution.py:130
  425.0 1.2 copy-start.3
  425.0 7.2 slice-start
  426.2 6.0 slice-start.1
  426.2 6.7 slice-start.2
  426.2 6.9 copy-start.5
  436.6 48.0 %collective-permute-start.2 = (bf16[16,1,17,768]{3,0,2,1:T(8,128)(2,1)}, bf16[16,1,17,768]{3,0,2,1:T(8,128)(2,1)S(1)}, u32[]{:S(2)}, u32[]{:S(2)}) collective-permute-start(bf16[16,1,17,768]{3,0,2,1:T(8,128)(2,1)} %get-tuple-element.24), channel_id=1, source_target_pairs={{0,12},{4,0},{8,4},{12,8},{1,13},{5,1},{9,5},{13,9},{2,14},{6,2},{... | collective-permute-start | bytes 1253384 | tf_op jit(solution)/shard_map/ppermute | solution.py:25
  440.1 44.4 %collective-permute-start.1 = (bf16[16,1,17,768]{3,0,2,1:T(8,128)(2,1)}, bf16[16,1,17,768]{3,0,2,1:T(8,128)(2,1)S(1)}, u32[]{:S(2)}, u32[]{:S(2)}) collective-permute-start(bf16[16,1,17,768]{3,0,2,1:T(8,128)(2,1)} %get-tuple-element.25), channel_id=1, source_target_pairs={{0,8},{4,12},{8,0},{12,4},{1,9},{5,13},{9,1},{13,5},{2,10},{6,14},... | collective-permute-start | bytes 1253384 | tf_op jit(solution)/shard_map/ppermute | solution.py:25
  440.1 44.4 %collective-permute-start = (bf16[16,1,17,768]{3,0,2,1:T(8,128)(2,1)}, bf16[16,1,17,768]{3,0,2,1:T(8,128)(2,1)}, u32[]{:S(2)}, u32[]{:S(2)}) collective-permute-start(bf16[16,1,17,768]{3,0,2,1:T(8,128)(2,1)} %get-tuple-element.26), channel_id=1, source_target_pairs={{0,4},{4,8},{8,12},{12,0},{1,5},{5,9},{9,13},{13,1},{2,6},{6,10},{... | collective-permute-start | bytes 1253384 | tf_op jit(solution)/shard_map/ppermute | solution.py:25
  442.9 33.9 %all-to-all-start.3 = ((bf16[4,2,136]{2,1,0:T(2,128)(2,1)}), bf16[4,2,136]{2,1,0:T(2,128)(2,1)S(1)}, u32[]{:S(2)}, u32[]{:S(2)}) async-start(bf16[4,2,136]{2,1,0:T(2,128)(2,1)} %reshape.341), calls=%async_computation.3 | async-start | bytes 8192 | tf_op jit(solution)/shard_map/all_to_all | solution.py:104
  484.6 0.8 copy-start.6
  492.2 254.1 %copy-start.1 = (bf16[128,768]{1,0:T(8,128)(2,1)S(1)}, bf16[128,768]{1,0:T(8,128)(2,1)}, u32[]{:S(2)}) copy-start(bf16[128,768]{1,0:T(8,128)(2,1)} %param.7) | copy-start | bytes 589828
Sparse Core Ops, SparseCore 0:
  9.6 120.6 all-gather.5
  131.8 117.9 all-gather.7
  251.4 117.8 all-gather.3
  376.9 22.4 all-reduce.2
  407.8 111.6 reduce-scatter.3
  522.3 110.5 reduce-scatter.5
  635.8 110.5 reduce-scatter.7
